TPU v7x, 512 devices: a whole 4x8x8 slice. The times are simulated.
512 devices in a mesh: mem: 4 (over x), lat: 4 (over y_hi, core), lon: 32 (over z, y_lo).
Axes of the slice: x: 4, y: 8 (y_hi: 2, y_lo: 4; y = y_hi * 4 + y_lo), z: 8, core: 2. Of those that a mesh axis runs over, the one named last changes fastest.
Arguments:
- initial_temp: float32 [100, 128, 512], P(None, 'lon', 'lat'), may hold values from -6 to 6
- land_mask: int32 [128, 512], P('lon', 'lat'), may hold values 0 or 1
- pert_table: float32 [16, 100], replicated, may hold values from 0.03 to 0.24
- pert_index: int32 [8], P('mem'), may hold values from 0 to 15
- base_kh: float32 [100], replicated, may hold values from 0.03 to 0.24
- member_mix: bfloat16 [8, 100, 100], P('mem'), may hold values from -0.15625 to 0.15625
- base_mix: bfloat16 [100, 100], replicated, may hold values from -0.15625 to 0.15625
- owner: int32 [32768, 1], P(('lat', 'lon')), may hold values from 0 to 127; in each aligned block of 256 rows (0 to 255, 256 to 511, ...) at most 4 rows name the same one
- column: int32 [32768], P(('lat', 'lon')), may hold values from 0 to 511
- interp_w: float32 [32768, 100], P(('lat', 'lon')), may hold values from 0 to 1
- obs_inv_var: float32 [32768, 100], P(('lat', 'lon')), may hold values from 1 to 16
- observed: float32 [32768, 100], P(('lat', 'lon')), may hold values from -6 to 6
Outputs:
- member_temp: bfloat16 [8, 100, 128, 512], P('mem', None, 'lon', 'lat')
- base_temp: bfloat16 [100, 128, 512], P(None, 'lon', 'lat')
- gram_block: float32 [8, 8], replicated
- projection: float32 [8], replicated
- misfit: float32 [32768, 100], P(('lat', 'lon'))
Inputs may be any that keep to these rules, and one draw needn't show every extreme that they name: Within the records of one device no owner is named more than 4 times, and in every draw some owner is named exactly 4 times by some device's records. The column within the owner's block is the longitude offset times 128 plus the latitude offset.
All inputs are finite; a program needn't handle non-finite values. No bound on the sum of `land_mask` on one device may be relied on, other than what follows from the above.
Results may differ from a plain program's by a relative error of at most 0.012.
Values may be sent and summed in bfloat16 or wider, within the bound.
No kernel may reach another device: no remote copies, remote signals or barrier semaphores. Data moves between devices by JAX's collectives and lax.ppermute only.
A program may use at most 64 MiB of HBM per device.

v0:
```python
import jax
import jax.numpy as jnp
from jax import lax
from jax.sharding import PartitionSpec as P

STEPS = 5


def padded_2(cells, sides, width, closed):
    for axis, dim in sides:
        count = lax.axis_size(axis)
        ends = count if closed else count - 1
        head = lax.slice_in_dim(cells, 0, width, axis=dim)
        tail = lax.slice_in_dim(cells, cells.shape[dim] - width, cells.shape[dim], axis=dim)
        cells = jnp.concatenate(
            [
                lax.ppermute(tail, axis, [(i, (i + 1) % count) for i in range(ends)]),
                cells,
                lax.ppermute(head, axis, [((i + 1) % count, i) for i in range(ends)]),
            ],
            axis=dim,
        )
    return cells


def on_device(
    initial_temp,
    land_mask,
    pert_table,
    pert_index,
    base_kh,
    member_mix,
    base_mix,
    owner,
    column,
    interp_w,
    obs_inv_var,
    observed,
):
    members = pert_index.shape[0]
    levels = initial_temp.shape[0]
    width_lon = initial_temp.shape[1]
    width_lat = initial_temp.shape[2]
    table_rows = pert_table.shape[0]
    chooser = (pert_index[:, None] == jnp.arange(table_rows)[None, :]).astype(jnp.float32)
    member_kh = jnp.dot(chooser, pert_table, precision=lax.Precision.HIGHEST)
    run_kh = jnp.concatenate([member_kh, base_kh[None, :]], 0)
    run_mix = jnp.concatenate([member_mix, base_mix[None]], 0)
    run_count = members + 1
    fields = jnp.broadcast_to(
        initial_temp.astype(jnp.bfloat16)[None], (run_count, levels, width_lon, width_lat)
    )
    total_lat = width_lat * lax.axis_size("lat")
    lat_start = lax.axis_index("lat") * width_lat
    ocean_open = land_mask.astype(jnp.float32)
    for step_index in range(STEPS):
        lon_padded = padded_2(fields, (("lon", 2),), 1, True)
        padded = padded_2(lon_padded, (("lat", 3),), 1, False)
        global_rows = lat_start - (1 - 1) + jnp.arange(width_lat + 2 * (1 - 1))
        has_next = (global_rows < total_lat - 1).astype(jnp.float32)
        has_prior = (global_rows > 0).astype(jnp.float32)
        widened = padded.astype(jnp.float32)
        values = widened[:, :, 1:-1, 1:-1]
        laplace = widened[:, :, 2:, 1:-1] + widened[:, :, :-2, 1:-1] - 2.0 * values
        laplace = (
            laplace
            + has_next * (widened[:, :, 1:-1, 2:] - values)
            + has_prior * (widened[:, :, 1:-1, :-2] - values)
        )
        right_side = (values + run_kh[:, :, None, None] * laplace).astype(jnp.bfloat16)
        vertical = right_side.astype(jnp.float32) + jnp.einsum(
            "rkj,rjab->rkab", run_mix, right_side, preferred_element_type=jnp.float32
        )
        fields = (values + ocean_open * (vertical - values)).astype(jnp.bfloat16)
    owners = lax.axis_size("lat") * lax.axis_size("lon")
    prof_dev = owner.shape[0]
    capacity = max(2, 2 * prof_dev // owners)
    target = owner[:, 0]
    matches = (target[:, None] == jnp.arange(owners)[None, :]).astype(jnp.int32)
    earlier = jnp.cumsum(matches, 0) - matches
    slot_rank = jnp.sum(earlier * matches, 1)
    position = target * capacity + slot_rank
    send_ids = (
        jnp.full((owners * capacity,), -1, jnp.int32)
        .at[position]
        .set(column)
        .reshape(owners, capacity)
    )
    records = jnp.stack([interp_w, obs_inv_var, observed], 1)
    send_records = (
        jnp.zeros((owners * capacity, 3, levels), jnp.float32)
        .at[position]
        .set(records)
        .reshape(owners, capacity, 3, levels)
    )
    columns_flat = fields.reshape(run_count, levels, width_lon * width_lat)
    column_ids = lax.all_to_all(send_ids, ("lat", "lon"), split_axis=0, concat_axis=0, tiled=True)
    record_rows = lax.all_to_all(
        send_records, ("lat", "lon"), split_axis=0, concat_axis=0, tiled=True
    )
    sources = column_ids.shape[0]
    slot_count = column_ids.shape[1]
    usable = (column_ids >= 0).astype(jnp.float32).reshape(-1)
    picked = jnp.take(columns_flat, jnp.maximum(column_ids, 0).reshape(-1), axis=2).astype(
        jnp.float32
    )
    deeper = jnp.concatenate([picked[:, 1:], picked[:, -1:]], 1)
    flat_records = record_rows.reshape(sources * slot_count, 3, levels)
    weight = flat_records[:, 0].T
    inv_var = flat_records[:, 1].T * usable
    measured = flat_records[:, 2].T
    modeled = weight * picked + (1.0 - weight) * deeper
    green_cols = ((modeled[:members] - modeled[members]) * usable).astype(jnp.bfloat16)
    misfit = (measured - modeled[members]) * usable
    extras = jnp.stack([inv_var, misfit], 0)
    green_cols, extras = (
        green_cols.reshape(members, levels, sources, slot_count),
        extras.reshape(2, levels, sources, slot_count),
    )
    owner_misfit = jnp.transpose(extras[1], (1, 2, 0))
    returned = lax.all_to_all(owner_misfit, ("lat", "lon"), split_axis=0, concat_axis=0, tiled=True)
    misfit_rows = jnp.take(returned.reshape(owners * capacity, levels), position, axis=0)
    green_cols = green_cols.reshape(members, levels, -1)
    extras = extras.reshape(2, levels, -1)
    normalizer = 1.0 / (prof_dev * owners * levels)
    green_all = lax.all_gather(green_cols, "mem", axis=0, tiled=True)
    green_float = green_all.astype(jnp.float32)
    weighted = green_float * extras[0]
    gram_part = (
        jnp.einsum("mks,nks->mn", weighted, green_float, precision=lax.Precision.HIGHEST)
        * normalizer
    )
    proj_part = (
        jnp.einsum("mks,ks->m", weighted, extras[1], precision=lax.Precision.HIGHEST) * normalizer
    )
    gram_part, proj_part = (gram_part, proj_part)
    gram_block, projection = lax.psum((gram_part, proj_part), ("lat", "lon"))
    return (fields[:members], fields[members], gram_block, projection, misfit_rows)


def solution(mesh):
    placed = (
        P(None, "lon", "lat"),
        P("lon", "lat"),
        P(),
        P("mem"),
        P(),
        P("mem", None, None),
        P(),
        P(("lat", "lon"), None),
        P(("lat", "lon")),
        P(("lat", "lon"), None),
        P(("lat", "lon"), None),
        P(("lat", "lon"), None),
    )
    return jax.shard_map(
        on_device,
        mesh=mesh,
        in_specs=placed,
        out_specs=(
            P("mem", None, "lon", "lat"),
            P(None, "lon", "lat"),
            P(),
            P(),
            P(("lat", "lon"), None),
        ),
        check_vma=False,
    )
```

profile of v0, /device:TPU:258, one launch (start us, length us, event | category | flops | bytes accessed | tf_op | source)
XLA Modules:
  0.0 559.3 jit_solution(4841442048766482967)
XLA Ops:
  1.6 4.6 collective-permute-start.1
  6.3 1.9 collective-permute-start
  10.8 5.7 %collective-permute-done = bf16[3,100,1,128]{3,1,2,0:T(8,128)(2,1)S(1)} collective-permute-done((bf16[3,100,1,128]{3,1,2,0:T(8,128)(2,1)S(1)}, bf16[3,100,1,128]{3,1,2,0:T(8,128)(2,1)S(1)}, u32[]{:S(2)}, u32[]{:S(2)}) %collective-permute-start) | collective-permute-done | bytes 76832 | tf_op jit(solution)/shard_map/ppermute | solution.py:17
  19.6 5.7 %collective-permute-done.3 = bf16[3,100,6,1]{3,1,2,0:T(8,128)(2,1)S(1)} collective-permute-done((bf16[3,100,6,1]{3,1,2,0:T(8,128)(2,1)S(1)}, bf16[3,100,6,1]{3,1,2,0:T(8,128)(2,1)S(1)}, u32[]{:S(2)}, u32[]{:S(2)}) %collective-permute-start.3) | collective-permute-done | bytes 3632 | tf_op jit(solution)/shard_map/ppermute | solution.py:19
  27.4 1.9 collective-permute-start.4
  29.4 7.8 %collective-permute-start.5 = (bf16[3,100,1,128]{3,1,2,0:T(8,128)(2,1)S(1)}, bf16[3,100,1,128]{3,1,2,0:T(8,128)(2,1)S(1)}, u32[]{:S(2)}, u32[]{:S(2)}) collective-permute-start(bf16[3,100,1,128]{3,1,2,0:T(8,128)(2,1)S(1)} %get-tuple-element.41), channel_id=1, source_target_pairs={{1,0},{2,1},{3,2},{4,3},{5,4},{6,5},{7,6},{8,7},{9,8},{10,9},{11,1... | collective-permute-start | bytes 230408 | tf_op jit(solution)/shard_map/ppermute | solution.py:19
  39.5 13.3 %collective-permute-start.6 = (bf16[3,100,6,1]{3,1,2,0:T(8,128)(2,1)S(1)}, bf16[3,100,6,1]{3,1,2,0:T(8,128)(2,1)S(1)}, u32[]{:S(2)}, u32[]{:S(2)}) collective-permute-start(bf16[3,100,6,1]{3,1,2,0:T(8,128)(2,1)S(1)} %get-tuple-element.30), channel_id=1, source_target_pairs={{0,32},{32,64},{64,96},{1,33},{33,65},{65,97},{2,34},{34,66},{66,9... | collective-permute-start | bytes 10808 | tf_op jit(solution)/shard_map/ppermute | solution.py:17
  56.4 18.1 %all-to-all-start.1 = ((s32[128,1,4]{2,1,0:T(1,128)}), s32[128,1,4]{2,1,0:T(1,128)S(1)}, u32[]{:S(2)}, u32[]{:S(2)}) async-start(s32[128,1,4]{2,1,0:T(1,128)} %bitcast.22), calls=%async_computation.1 | async-start | bytes 131072 | tf_op jit(solution)/shard_map/all_to_all | solution.py:97
  75.2 1.6 fusion.20
  76.8 3.4 collective-permute-start.8
  80.2 6.4 %collective-permute-start.9 = (bf16[3,100,1,128]{3,1,2,0:T(8,128)(2,1)S(1)}, bf16[3,100,1,128]{3,1,2,0:T(8,128)(2,1)S(1)}, u32[]{:S(2)}, u32[]{:S(2)}) collective-permute-start(bf16[3,100,1,128]{3,1,2,0:T(8,128)(2,1)S(1)} %get-tuple-element.39), channel_id=1, source_target_pairs={{1,0},{2,1},{3,2},{4,3},{5,4},{6,5},{7,6},{8,7},{9,8},{10,9},{11,1... | collective-permute-start | bytes 230408 | tf_op jit(solution)/shard_map/ppermute | solution.py:19
  93.0 7.1 %scatter_fusion = f32[512,3,100]{2,1,0:T(4,128)S(1)} fusion(f32[512,3,100]{2,1,0:T(4,128)S(1)} %broadcast_in_dim.33, s32[256]{0:T(256)S(1)} %bitcast.104, f32[256,3,100]{2,1,0:T(4,128)S(1)} %copy.45), kind=kCustom, calls=%fused_computation.2 | custom fusion | bytes 922624 | tf_op jit(solution)/shard_map/scatter | solution.py:93
  103.3 1.9 collective-permute-start.12
  105.2 8.2 %collective-permute-start.13 = (bf16[3,100,1,128]{3,1,2,0:T(8,128)(2,1)S(1)}, bf16[3,100,1,128]{3,1,2,0:T(8,128)(2,1)S(1)}, u32[]{:S(2)}, u32[]{:S(2)}) collective-permute-start(bf16[3,100,1,128]{3,1,2,0:T(8,128)(2,1)S(1)} %get-tuple-element.37), channel_id=1, source_target_pairs={{1,0},{2,1},{3,2},{4,3},{5,4},{6,5},{7,6},{8,7},{9,8},{10,9},{11,1... | collective-permute-start | bytes 230408 | tf_op jit(solution)/shard_map/ppermute | solution.py:19
  113.4 21.5 %all-to-all-start = ((f32[128,4,3,100]{3,1,2,0:T(4,128)}), f32[128,4,3,100]{3,1,2,0:T(4,128)S(1)}, u32[]{:S(2)}, u32[]{:S(2)}) async-start(f32[128,4,3,100]{3,1,2,0:T(4,128)} %copy.47), calls=%async_computation | async-start | bytes 1572864 | tf_op jit(solution)/shard_map/all_to_all | solution.py:98
  135.5 2.3 collective-permute-start.14
  140.1 6.5 %collective-permute-done.15 = bf16[3,100,6,1]{3,1,2,0:T(8,128)(2,1)} collective-permute-done((bf16[3,100,6,1]{3,1,2,0:T(8,128)(2,1)S(1)}, bf16[3,100,6,1]{3,1,2,0:T(8,128)(2,1)}, u32[]{:S(2)}, u32[]{:S(2)}) %collective-permute-start.15) | collective-permute-done | bytes 3632 | tf_op jit(solution)/shard_map/ppermute | solution.py:19
  146.7 1.7 maximum_convert_fusion.3
  150.0 2.5 collective-permute-start.16
  152.5 7.3 %collective-permute-start.17 = (bf16[3,100,1,128]{3,1,2,0:T(8,128)(2,1)S(1)}, bf16[3,100,1,128]{3,1,2,0:T(8,128)(2,1)S(1)}, u32[]{:S(2)}, u32[]{:S(2)}) collective-permute-start(bf16[3,100,1,128]{3,1,2,0:T(8,128)(2,1)S(1)} %get-tuple-element.35), channel_id=1, source_target_pairs={{1,0},{2,1},{3,2},{4,3},{5,4},{6,5},{7,6},{8,7},{9,8},{10,9},{11,1... | collective-permute-start | bytes 230408 | tf_op jit(solution)/shard_map/ppermute | solution.py:19
  160.0 1.6 collective-permute-done.16
  162.1 23.8 %collective-permute-start.18 = (bf16[3,100,6,1]{3,1,2,0:T(8,128)(2,1)S(1)}, bf16[3,100,6,1]{3,1,2,0:T(8,128)(2,1)S(1)}, u32[]{:S(2)}, u32[]{:S(2)}) collective-permute-start(bf16[3,100,6,1]{3,1,2,0:T(8,128)(2,1)S(1)} %get-tuple-element.24), channel_id=1, source_target_pairs={{0,32},{32,64},{64,96},{1,33},{33,65},{65,97},{2,34},{34,66},{66,9... | collective-permute-start | bytes 10808 | tf_op jit(solution)/shard_map/ppermute | solution.py:17
  188.5 1.7 collective-permute-done.19
  190.2 1.7 maximum_convert_fusion.4
  194.3 2.1 gather_fusion
  196.4 1.8 convert_bitcast_fusion
  201.2 1.9 fusion.36
  206.1 24.3 %all-to-all-start.2 = ((f32[128,4,100]{2,1,0:T(4,128)}), f32[128,4,100]{2,1,0:T(4,128)S(1)}, u32[]{:S(2)}, u32[]{:S(2)}) async-start(f32[128,4,100]{2,1,0:T(4,128)} %bitcast.35), calls=%async_computation.2 | async-start | bytes 524288 | tf_op jit(solution)/shard_map/all_to_all | solution.py:121
  231.5 14.8 %all_gather.3 = bf16[8,100,512]{2,1,0:T(8,128)(2,1)S(1)} all-gather(bf16[2,100,512]{2,1,0:T(8,128)(2,1)S(1)} %copy.52), channel_id=1, replica_groups=mesh['mem'=4,'lat'=4,'lon'=32] {'mem'}, dimensions={0}, use_global_device_ids=true | all-gather | bytes 1024000 | tf_op jit(solution)/shard_map/all_gather | solution.py:126
  246.6 3.9 fusion.33
  250.4 2.6 fusion.27
  253.0 304.7 %all-reduce = (f32[8,8]{1,0:T(8,128)}, f32[8]{0:T(128)}) all-reduce(f32[8,8]{1,0:T(8,128)S(1)} %fusion.27, f32[8]{0:T(128)S(1)} %fusion.33), channel_id=1, replica_groups=mesh['mem'=4,'lat'=4,'lon'=32] {'lat','lon'}, use_global_device_ids=true, to_apply=%region_5.6 | all-reduce | flops 72 | bytes 576 | tf_op jit(solution)/shard_map/psum | solution.py:137
  (126 shorter events, 43.7 us)
Async XLA Ops:
  0.6 8.6 %copy-start = (f32[16,100]{1,0:T(8,128)S(1)}, f32[16,100]{1,0:T(8,128)}, u32[]{:S(2)}) copy-start(f32[16,100]{1,0:T(8,128)} %param.14) | copy-start | bytes 19204
  1.6 9.2 %collective-permute-start.1 = (bf16[3,100,1,128]{3,1,2,0:T(8,128)(2,1)S(1)}, bf16[3,100,1,128]{3,1,2,0:T(8,128)(2,1)S(1)}, u32[]{:S(2)}, u32[]{:S(2)}) collective-permute-start(bf16[3,100,1,128]{3,1,2,0:T(8,128)(2,1)S(1)} %broadcast_in_dim.30), channel_id=1, source_target_pairs={{1,0},{2,1},{3,2},{4,3},{5,4},{6,5},{7,6},{8,7},{9,8},{10,9},{11,1... | collective-permute-start | bytes 230408 | tf_op jit(solution)/shard_map/ppermute | solution.py:19
  6.3 10.2 %collective-permute-start = (bf16[3,100,1,128]{3,1,2,0:T(8,128)(2,1)S(1)}, bf16[3,100,1,128]{3,1,2,0:T(8,128)(2,1)S(1)}, u32[]{:S(2)}, u32[]{:S(2)}) collective-permute-start(bf16[3,100,1,128]{3,1,2,0:T(8,128)(2,1)S(1)} %broadcast_in_dim.28), channel_id=1, source_target_pairs={{0,1},{1,2},{2,3},{3,4},{4,5},{5,6},{6,7},{7,8},{8,9},{9,10},{10,1... | collective-permute-start | bytes 230408 | tf_op jit(solution)/shard_map/ppermute | solution.py:17
  9.0 10.5 %copy-start.10 = (s32[4,128]{1,0:T(4,128)S(1)}, s32[4,128]{1,0:T(4,128)}, u32[]{:S(2)}) copy-start(s32[4,128]{1,0:T(4,128)} %param.13) | copy-start | bytes 6148
  9.0 10.5 %copy-start.8 = (bf16[2,100,100]{2,0,1:T(2,128)(2,1)S(1)}, bf16[2,100,100]{2,0,1:T(2,128)(2,1)}, u32[]{:S(2)}) copy-start(bf16[2,100,100]{2,0,1:T(2,128)(2,1)} %param.17) | copy-start | bytes 120004
  16.8 9.0 %copy-start.11 = (bf16[100,100]{1,0:T(8,128)(2,1)S(1)}, bf16[100,100]{1,0:T(8,128)(2,1)}, u32[]{:S(2)}) copy-start(bf16[100,100]{1,0:T(8,128)(2,1)} %param.18) | copy-start | bytes 60004
  16.8 2.8 collective-permute-start.2
  18.1 7.1 %collective-permute-start.3 = (bf16[3,100,6,1]{3,1,2,0:T(8,128)(2,1)S(1)}, bf16[3,100,6,1]{3,1,2,0:T(8,128)(2,1)S(1)}, u32[]{:S(2)}, u32[]{:S(2)}) collective-permute-start(bf16[3,100,6,1]{3,1,2,0:T(8,128)(2,1)S(1)} %get-tuple-element.33), channel_id=1, source_target_pairs={{32,0},{64,32},{96,64},{33,1},{65,33},{97,65},{34,2},{66,34},{98,6... | collective-permute-start | bytes 10808 | tf_op jit(solution)/shard_map/ppermute | solution.py:19
  25.8 11.4 %copy-start.9 = (s32[256,1]{0,1:T(1,128)S(1)}, s32[256,1]{0,1:T(1,128)}, u32[]{:S(2)}) copy-start(s32[256,1]{0,1:T(1,128)} %param.19) | copy-start | bytes 3076
  27.4 10.2 %collective-permute-start.4 = (bf16[3,100,1,128]{3,1,2,0:T(8,128)(2,1)S(1)}, bf16[3,100,1,128]{3,1,2,0:T(8,128)(2,1)S(1)}, u32[]{:S(2)}, u32[]{:S(2)}) collective-permute-start(bf16[3,100,1,128]{3,1,2,0:T(8,128)(2,1)S(1)} %get-tuple-element.40), channel_id=1, source_target_pairs={{0,1},{1,2},{2,3},{3,4},{4,5},{5,6},{6,7},{7,8},{8,9},{9,10},{10,1... | collective-permute-start | bytes 230408 | tf_op jit(solution)/shard_map/ppermute | solution.py:17
  29.4 9.9 %collective-permute-start.5 = (bf16[3,100,1,128]{3,1,2,0:T(8,128)(2,1)S(1)}, bf16[3,100,1,128]{3,1,2,0:T(8,128)(2,1)S(1)}, u32[]{:S(2)}, u32[]{:S(2)}) collective-permute-start(bf16[3,100,1,128]{3,1,2,0:T(8,128)(2,1)S(1)} %get-tuple-element.41), channel_id=1, source_target_pairs={{1,0},{2,1},{3,2},{4,3},{5,4},{6,5},{7,6},{8,7},{9,8},{10,9},{11,1... | collective-permute-start | bytes 230408 | tf_op jit(solution)/shard_map/ppermute | solution.py:19
  39.5 35.1 %collective-permute-start.6 = (bf16[3,100,6,1]{3,1,2,0:T(8,128)(2,1)S(1)}, bf16[3,100,6,1]{3,1,2,0:T(8,128)(2,1)S(1)}, u32[]{:S(2)}, u32[]{:S(2)}) collective-permute-start(bf16[3,100,6,1]{3,1,2,0:T(8,128)(2,1)S(1)} %get-tuple-element.30), channel_id=1, source_target_pairs={{0,32},{32,64},{64,96},{1,33},{33,65},{65,97},{2,34},{34,66},{66,9... | collective-permute-start | bytes 10808 | tf_op jit(solution)/shard_map/ppermute | solution.py:17
  52.8 21.8 %collective-permute-start.7 = (bf16[3,100,6,1]{3,1,2,0:T(8,128)(2,1)S(1)}, bf16[3,100,6,1]{3,1,2,0:T(8,128)(2,1)S(1)}, u32[]{:S(2)}, u32[]{:S(2)}) collective-permute-start(bf16[3,100,6,1]{3,1,2,0:T(8,128)(2,1)S(1)} %get-tuple-element.31), channel_id=1, source_target_pairs={{32,0},{64,32},{96,64},{33,1},{65,33},{97,65},{34,2},{66,34},{98,6... | collective-permute-start | bytes 10808 | tf_op jit(solution)/shard_map/ppermute | solution.py:19
  56.4 57.0 %all-to-all-start.1 = ((s32[128,1,4]{2,1,0:T(1,128)}), s32[128,1,4]{2,1,0:T(1,128)S(1)}, u32[]{:S(2)}, u32[]{:S(2)}) async-start(s32[128,1,4]{2,1,0:T(1,128)} %bitcast.22), calls=%async_computation.1 | async-start | bytes 131072 | tf_op jit(solution)/shard_map/all_to_all | solution.py:97
  75.1 11.4 %copy-start.5 = (f32[256,100]{0,1:T(8,128)S(1)}, f32[256,100]{0,1:T(8,128)}, u32[]{:S(2)}) copy-start(f32[256,100]{0,1:T(8,128)} %param.23) | copy-start | bytes 307204
  75.1 11.4 %copy-start.6 = (f32[256,100]{0,1:T(8,128)S(1)}, f32[256,100]{0,1:T(8,128)}, u32[]{:S(2)}) copy-start(f32[256,100]{0,1:T(8,128)} %param.22) | copy-start | bytes 307204
  75.1 11.4 %copy-start.7 = (f32[256,100]{0,1:T(8,128)S(1)}, f32[256,100]{0,1:T(8,128)}, u32[]{:S(2)}) copy-start(f32[256,100]{0,1:T(8,128)} %param.21) | copy-start | bytes 307204
  76.8 10.5 %collective-permute-start.8 = (bf16[3,100,1,128]{3,1,2,0:T(8,128)(2,1)S(1)}, bf16[3,100,1,128]{3,1,2,0:T(8,128)(2,1)S(1)}, u32[]{:S(2)}, u32[]{:S(2)}) collective-permute-start(bf16[3,100,1,128]{3,1,2,0:T(8,128)(2,1)S(1)} %get-tuple-element.38), channel_id=1, source_target_pairs={{0,1},{1,2},{2,3},{3,4},{4,5},{5,6},{6,7},{7,8},{8,9},{9,10},{10,1... | collective-permute-start | bytes 230408 | tf_op jit(solution)/shard_map/ppermute | solution.py:17
  80.2 8.4 %collective-permute-start.9 = (bf16[3,100,1,128]{3,1,2,0:T(8,128)(2,1)S(1)}, bf16[3,100,1,128]{3,1,2,0:T(8,128)(2,1)S(1)}, u32[]{:S(2)}, u32[]{:S(2)}) collective-permute-start(bf16[3,100,1,128]{3,1,2,0:T(8,128)(2,1)S(1)} %get-tuple-element.39), channel_id=1, source_target_pairs={{1,0},{2,1},{3,2},{4,3},{5,4},{6,5},{7,6},{8,7},{9,8},{10,9},{11,1... | collective-permute-start | bytes 230408 | tf_op jit(solution)/shard_map/ppermute | solution.py:19
  89.8 11.4 %collective-permute-start.10 = (bf16[3,100,6,1]{3,1,2,0:T(8,128)(2,1)}, bf16[3,100,6,1]{3,1,2,0:T(8,128)(2,1)S(1)}, u32[]{:S(2)}, u32[]{:S(2)}) collective-permute-start(bf16[3,100,6,1]{3,1,2,0:T(8,128)(2,1)} %get-tuple-element.28), channel_id=1, source_target_pairs={{0,32},{32,64},{64,96},{1,33},{33,65},{65,97},{2,34},{34,66},{66,9... | collective-permute-start | bytes 10808 | tf_op jit(solution)/shard_map/ppermute | solution.py:17
  91.1 10.1 %collective-permute-start.11 = (bf16[3,100,6,1]{3,1,2,0:T(8,128)(2,1)}, bf16[3,100,6,1]{3,1,2,0:T(8,128)(2,1)S(1)}, u32[]{:S(2)}, u32[]{:S(2)}) collective-permute-start(bf16[3,100,6,1]{3,1,2,0:T(8,128)(2,1)} %get-tuple-element.29), channel_id=1, source_target_pairs={{32,0},{64,32},{96,64},{33,1},{65,33},{97,65},{34,2},{66,34},{98,6... | collective-permute-start | bytes 10808 | tf_op jit(solution)/shard_map/ppermute | solution.py:19
  103.3 31.9 %collective-permute-start.12 = (bf16[3,100,1,128]{3,1,2,0:T(8,128)(2,1)S(1)}, bf16[3,100,1,128]{3,1,2,0:T(8,128)(2,1)S(1)}, u32[]{:S(2)}, u32[]{:S(2)}) collective-permute-start(bf16[3,100,1,128]{3,1,2,0:T(8,128)(2,1)S(1)} %get-tuple-element.36), channel_id=1, source_target_pairs={{0,1},{1,2},{2,3},{3,4},{4,5},{5,6},{6,7},{7,8},{8,9},{9,10},{10,1... | collective-permute-start | bytes 230408 | tf_op jit(solution)/shard_map/ppermute | solution.py:17
  105.2 30.0 %collective-permute-start.13 = (bf16[3,100,1,128]{3,1,2,0:T(8,128)(2,1)S(1)}, bf16[3,100,1,128]{3,1,2,0:T(8,128)(2,1)S(1)}, u32[]{:S(2)}, u32[]{:S(2)}) collective-permute-start(bf16[3,100,1,128]{3,1,2,0:T(8,128)(2,1)S(1)} %get-tuple-element.37), channel_id=1, source_target_pairs={{1,0},{2,1},{3,2},{4,3},{5,4},{6,5},{7,6},{8,7},{9,8},{10,9},{11,1... | collective-permute-start | bytes 230408 | tf_op jit(solution)/shard_map/ppermute | solution.py:19
  113.4 87.4 %all-to-all-start = ((f32[128,4,3,100]{3,1,2,0:T(4,128)}), f32[128,4,3,100]{3,1,2,0:T(4,128)S(1)}, u32[]{:S(2)}, u32[]{:S(2)}) async-start(f32[128,4,3,100]{3,1,2,0:T(4,128)} %copy.47), calls=%async_computation | async-start | bytes 1572864 | tf_op jit(solution)/shard_map/all_to_all | solution.py:98
  135.5 3.9 collective-permute-start.14
  137.8 8.9 %collective-permute-start.15 = (bf16[3,100,6,1]{3,1,2,0:T(8,128)(2,1)S(1)}, bf16[3,100,6,1]{3,1,2,0:T(8,128)(2,1)}, u32[]{:S(2)}, u32[]{:S(2)}) collective-permute-start(bf16[3,100,6,1]{3,1,2,0:T(8,128)(2,1)S(1)} %get-tuple-element.27), channel_id=1, source_target_pairs={{32,0},{64,32},{96,64},{33,1},{65,33},{97,65},{34,2},{66,34},{98,6... | collective-permute-start | bytes 10808 | tf_op jit(solution)/shard_map/ppermute | solution.py:19
  150.0 11.6 %collective-permute-start.16 = (bf16[3,100,1,128]{3,1,2,0:T(8,128)(2,1)S(1)}, bf16[3,100,1,128]{3,1,2,0:T(8,128)(2,1)S(1)}, u32[]{:S(2)}, u32[]{:S(2)}) collective-permute-start(bf16[3,100,1,128]{3,1,2,0:T(8,128)(2,1)S(1)} %get-tuple-element.34), channel_id=1, source_target_pairs={{0,1},{1,2},{2,3},{3,4},{4,5},{5,6},{6,7},{7,8},{8,9},{9,10},{10,1... | collective-permute-start | bytes 230408 | tf_op jit(solution)/shard_map/ppermute | solution.py:17
  152.5 9.4 %collective-permute-start.17 = (bf16[3,100,1,128]{3,1,2,0:T(8,128)(2,1)S(1)}, bf16[3,100,1,128]{3,1,2,0:T(8,128)(2,1)S(1)}, u32[]{:S(2)}, u32[]{:S(2)}) collective-permute-start(bf16[3,100,1,128]{3,1,2,0:T(8,128)(2,1)S(1)} %get-tuple-element.35), channel_id=1, source_target_pairs={{1,0},{2,1},{3,2},{4,3},{5,4},{6,5},{7,6},{8,7},{9,8},{10,9},{11,1... | collective-permute-start | bytes 230408 | tf_op jit(solution)/shard_map/ppermute | solution.py:19
  162.1 25.6 %collective-permute-start.18 = (bf16[3,100,6,1]{3,1,2,0:T(8,128)(2,1)S(1)}, bf16[3,100,6,1]{3,1,2,0:T(8,128)(2,1)S(1)}, u32[]{:S(2)}, u32[]{:S(2)}) collective-permute-start(bf16[3,100,6,1]{3,1,2,0:T(8,128)(2,1)S(1)} %get-tuple-element.24), channel_id=1, source_target_pairs={{0,32},{32,64},{64,96},{1,33},{33,65},{65,97},{2,34},{34,66},{66,9... | collective-permute-start | bytes 10808 | tf_op jit(solution)/shard_map/ppermute | solution.py:17
  186.0 4.2 collective-permute-start.19
  198.1 1.9 slice-start
  206.1 351.7 %all-to-all-start.2 = ((f32[128,4,100]{2,1,0:T(4,128)}), f32[128,4,100]{2,1,0:T(4,128)S(1)}, u32[]{:S(2)}, u32[]{:S(2)}) async-start(f32[128,4,100]{2,1,0:T(4,128)} %bitcast.35), calls=%async_computation.2 | async-start | bytes 524288 | tf_op jit(solution)/shard_map/all_to_all | solution.py:121
  (4 other events, 3.5 us)
where the time goes:
time: 560 us; the launch traced here: 559 us
  blocking collectives  320 us (57%)
  starting transfers between devices  159 us (28%)
  local copies, waits for them, and re-layouts  25.4 us (5%)
  waiting for transfers between devices  25.4 us (5%)
  matrix products  15.2 us (3%)
  other arithmetic  13.8 us (2%)
    psum x1, blocking collectives, on_device(): gram_block, projection = lax.psum((gram_part, proj_part), ('lat', 'lon'))  305 us
    ppermute x10, starting transfers between devices, padded_2(): lax.ppermute(tail, axis, [(i, (i + 1) % count) for i in range(ends)])  53.6 us
    ppermute x10, starting transfers between devices, padded_2(): lax.ppermute(head, axis, [((i + 1) % count, i) for i in range(ends)])  41.1 us
    all_to_all x1, starting transfers between devices, on_device(): lax.all_to_all(owner_misfit, ('lat', 'lon'), split_axis=0, concat_axis=0,...  24.3 us
    all_to_all x1, starting transfers between devices, on_device(): lax.all_to_all(send_records, ('lat', 'lon'), split_axis=0, concat_axis=0,...  21.5 us
    all_to_all x1, starting transfers between devices, on_device(): lax.all_to_all(send_ids, ('lat', 'lon'), split_axis=0, concat_axis=0, til...  18.1 us
    ppermute x10, waiting for transfers between devices, padded_2(): lax.ppermute(head, axis, [((i + 1) % count, i) for i in range(ends)])  17.1 us
    all_gather x1, blocking collectives, on_device(): green_all = lax.all_gather(green_cols, 'mem', axis=0, tiled=True)  14.8 us
  transfers between devices with their start and end apart: 23, of which 10 were waited for; matrix products, arithmetic and copies ran while one was open for 7% of the time, Pallas kernels for 0%

commit v1 on v0

--- a/solution.py
+++ b/solution.py
@@ -4,6 +4,11 @@
 from jax.sharding import PartitionSpec as P
 
 STEPS = 5
+
+
+def state_heaps(row_axis, axis_key, s0):
+    current_block = lax.psum(s0, axis_key)
+    return lax.psum(current_block, row_axis)
 
 
 def padded_2(cells, sides, width, closed):
@@ -134,7 +139,7 @@
         jnp.einsum("mks,ks->m", weighted, extras[1], precision=lax.Precision.HIGHEST) * normalizer
     )
     gram_part, proj_part = (gram_part, proj_part)
-    gram_block, projection = lax.psum((gram_part, proj_part), ("lat", "lon"))
+    gram_block, projection = state_heaps("lon", "lat", (gram_part, proj_part))
     return (fields[:members], fields[members], gram_block, projection, misfit_rows)
 
 

time: 560 us -> 352 us (0.63)
  the two profiles are of different devices: /device:TPU:258 before, /device:TPU:2 now
where the time goes in v1:
time: 352 us; the launch traced here: 351 us
  starting transfers between devices  162 us (46%)
  blocking collectives  107 us (30%)
  waiting for transfers between devices  25.8 us (7%)
  local copies, waits for them, and re-layouts  25.4 us (7%)
  matrix products  15.2 us (4%)
  other arithmetic  13.8 us (4%)
    psum x1, blocking collectives, state_heaps(): return lax.psum(current_block, row_axis)  79.6 us
    ppermute x10, starting transfers between devices, padded_2(): lax.ppermute(tail, axis, [(i, (i + 1) % count) for i in range(ends)])  51.2 us
    ppermute x10, starting transfers between devices, padded_2(): lax.ppermute(head, axis, [((i + 1) % count, i) for i in range(ends)])  50.9 us
    all_to_all x1, starting transfers between devices, on_device(): lax.all_to_all(owner_misfit, ('lat', 'lon'), split_axis=0, concat_axis=0,...  24.7 us
    all_to_all x1, starting transfers between devices, on_device(): lax.all_to_all(send_records, ('lat', 'lon'), split_axis=0, concat_axis=0,...  21.5 us
    ppermute x10, waiting for transfers between devices, padded_2(): lax.ppermute(head, axis, [((i + 1) % count, i) for i in range(ends)])  17.8 us
    all_gather x1, blocking collectives, on_device(): green_all = lax.all_gather(green_cols, 'mem', axis=0, tiled=True)  14.4 us
    all_to_all x1, starting transfers between devices, on_device(): lax.all_to_all(send_ids, ('lat', 'lon'), split_axis=0, concat_axis=0, til...  13.9 us
  transfers between devices with their start and end apart: 23, of which 10 were waited for; matrix products, arithmetic and copies ran while one was open for 12% of the time, Pallas kernels for 0%

profile of v1, /device:TPU:2, one launch (start us, length us, event | category | flops | bytes accessed | tf_op | source)
XLA Modules:
  0.0 350.7 jit_solution(8631989751260173944)
XLA Ops:
  1.6 14.0 %collective-permute-start.1 = (bf16[3,100,1,128]{3,1,2,0:T(8,128)(2,1)S(1)}, bf16[3,100,1,128]{3,1,2,0:T(8,128)(2,1)S(1)}, u32[]{:S(2)}, u32[]{:S(2)}) collective-permute-start(bf16[3,100,1,128]{3,1,2,0:T(8,128)(2,1)S(1)} %broadcast_in_dim.30), channel_id=1, source_target_pairs={{1,0},{2,1},{3,2},{4,3},{5,4},{6,5},{7,6},{8,7},{9,8},{10,9},{11,1... | collective-permute-start | bytes 230408 | tf_op jit(solution)/shard_map/ppermute | solution.py:24
  15.6 1.9 collective-permute-start
  20.2 5.7 %collective-permute-done = bf16[3,100,1,128]{3,1,2,0:T(8,128)(2,1)S(1)} collective-permute-done((bf16[3,100,1,128]{3,1,2,0:T(8,128)(2,1)S(1)}, bf16[3,100,1,128]{3,1,2,0:T(8,128)(2,1)S(1)}, u32[]{:S(2)}, u32[]{:S(2)}) %collective-permute-start) | collective-permute-done | bytes 76832 | tf_op jit(solution)/shard_map/ppermute | solution.py:22
  28.9 5.6 %collective-permute-done.3 = bf16[3,100,6,1]{3,1,2,0:T(8,128)(2,1)S(1)} collective-permute-done((bf16[3,100,6,1]{3,1,2,0:T(8,128)(2,1)S(1)}, bf16[3,100,6,1]{3,1,2,0:T(8,128)(2,1)S(1)}, u32[]{:S(2)}, u32[]{:S(2)}) %collective-permute-start.3) | collective-permute-done | bytes 3632 | tf_op jit(solution)/shard_map/ppermute | solution.py:24
  35.2 1.6 fusion.19
  36.8 1.9 collective-permute-start.4
  38.7 7.8 %collective-permute-start.5 = (bf16[3,100,1,128]{3,1,2,0:T(8,128)(2,1)S(1)}, bf16[3,100,1,128]{3,1,2,0:T(8,128)(2,1)S(1)}, u32[]{:S(2)}, u32[]{:S(2)}) collective-permute-start(bf16[3,100,1,128]{3,1,2,0:T(8,128)(2,1)S(1)} %get-tuple-element.43), channel_id=1, source_target_pairs={{1,0},{2,1},{3,2},{4,3},{5,4},{6,5},{7,6},{8,7},{9,8},{10,9},{11,1... | collective-permute-start | bytes 230408 | tf_op jit(solution)/shard_map/ppermute | solution.py:24
  48.9 12.1 %collective-permute-start.6 = (bf16[3,100,6,1]{3,1,2,0:T(8,128)(2,1)S(1)}, bf16[3,100,6,1]{3,1,2,0:T(8,128)(2,1)S(1)}, u32[]{:S(2)}, u32[]{:S(2)}) collective-permute-start(bf16[3,100,6,1]{3,1,2,0:T(8,128)(2,1)S(1)} %get-tuple-element.32), channel_id=1, source_target_pairs={{0,32},{32,64},{64,96},{1,33},{33,65},{65,97},{2,34},{34,66},{66,9... | collective-permute-start | bytes 10808 | tf_op jit(solution)/shard_map/ppermute | solution.py:22
  64.6 13.9 %all-to-all-start.1 = ((s32[128,1,4]{2,1,0:T(1,128)}), s32[128,1,4]{2,1,0:T(1,128)S(1)}, u32[]{:S(2)}, u32[]{:S(2)}) async-start(s32[128,1,4]{2,1,0:T(1,128)} %bitcast.22), calls=%async_computation.1 | async-start | bytes 131072 | tf_op jit(solution)/shard_map/all_to_all | solution.py:102
  80.7 3.0 collective-permute-start.8
  83.8 6.7 %collective-permute-start.9 = (bf16[3,100,1,128]{3,1,2,0:T(8,128)(2,1)S(1)}, bf16[3,100,1,128]{3,1,2,0:T(8,128)(2,1)S(1)}, u32[]{:S(2)}, u32[]{:S(2)}) collective-permute-start(bf16[3,100,1,128]{3,1,2,0:T(8,128)(2,1)S(1)} %get-tuple-element.41), channel_id=1, source_target_pairs={{1,0},{2,1},{3,2},{4,3},{5,4},{6,5},{7,6},{8,7},{9,8},{10,9},{11,1... | collective-permute-start | bytes 230408 | tf_op jit(solution)/shard_map/ppermute | solution.py:24
  97.0 7.1 %scatter_fusion = f32[512,3,100]{2,1,0:T(4,128)S(1)} fusion(f32[512,3,100]{2,1,0:T(4,128)S(1)} %broadcast_in_dim.33, s32[256]{0:T(256)S(1)} %bitcast.104, f32[256,3,100]{2,1,0:T(4,128)S(1)} %copy.45), kind=kCustom, calls=%fused_computation.2 | custom fusion | bytes 922624 | tf_op jit(solution)/shard_map/scatter | solution.py:98
  107.3 1.9 collective-permute-start.12
  109.2 8.2 %collective-permute-start.13 = (bf16[3,100,1,128]{3,1,2,0:T(8,128)(2,1)S(1)}, bf16[3,100,1,128]{3,1,2,0:T(8,128)(2,1)S(1)}, u32[]{:S(2)}, u32[]{:S(2)}) collective-permute-start(bf16[3,100,1,128]{3,1,2,0:T(8,128)(2,1)S(1)} %get-tuple-element.39), channel_id=1, source_target_pairs={{1,0},{2,1},{3,2},{4,3},{5,4},{6,5},{7,6},{8,7},{9,8},{10,9},{11,1... | collective-permute-start | bytes 230408 | tf_op jit(solution)/shard_map/ppermute | solution.py:24
  117.5 21.5 %all-to-all-start = ((f32[128,4,3,100]{3,1,2,0:T(4,128)}), f32[128,4,3,100]{3,1,2,0:T(4,128)S(1)}, u32[]{:S(2)}, u32[]{:S(2)}) async-start(f32[128,4,3,100]{3,1,2,0:T(4,128)} %copy.47), calls=%async_computation | async-start | bytes 1572864 | tf_op jit(solution)/shard_map/all_to_all | solution.py:103
  139.5 1.7 collective-permute-start.14
  143.5 6.7 %collective-permute-done.15 = bf16[3,100,6,1]{3,1,2,0:T(8,128)(2,1)} collective-permute-done((bf16[3,100,6,1]{3,1,2,0:T(8,128)(2,1)S(1)}, bf16[3,100,6,1]{3,1,2,0:T(8,128)(2,1)}, u32[]{:S(2)}, u32[]{:S(2)}) %collective-permute-start.15) | collective-permute-done | bytes 3632 | tf_op jit(solution)/shard_map/ppermute | solution.py:24
  150.3 1.7 maximum_convert_fusion.3
  153.6 2.5 collective-permute-start.16
  156.1 7.3 %collective-permute-start.17 = (bf16[3,100,1,128]{3,1,2,0:T(8,128)(2,1)S(1)}, bf16[3,100,1,128]{3,1,2,0:T(8,128)(2,1)S(1)}, u32[]{:S(2)}, u32[]{:S(2)}) collective-permute-start(bf16[3,100,1,128]{3,1,2,0:T(8,128)(2,1)S(1)} %get-tuple-element.37), channel_id=1, source_target_pairs={{1,0},{2,1},{3,2},{4,3},{5,4},{6,5},{7,6},{8,7},{9,8},{10,9},{11,1... | collective-permute-start | bytes 230408 | tf_op jit(solution)/shard_map/ppermute | solution.py:24
  166.0 23.5 %collective-permute-start.18 = (bf16[3,100,6,1]{3,1,2,0:T(8,128)(2,1)S(1)}, bf16[3,100,6,1]{3,1,2,0:T(8,128)(2,1)S(1)}, u32[]{:S(2)}, u32[]{:S(2)}) collective-permute-start(bf16[3,100,6,1]{3,1,2,0:T(8,128)(2,1)S(1)} %get-tuple-element.26), channel_id=1, source_target_pairs={{0,32},{32,64},{64,96},{1,33},{33,65},{65,97},{2,34},{34,66},{66,9... | collective-permute-start | bytes 10808 | tf_op jit(solution)/shard_map/ppermute | solution.py:22
  192.1 1.7 collective-permute-done.19
  193.8 1.7 maximum_convert_fusion.4
  197.8 2.1 gather_fusion
  199.9 1.8 convert_bitcast_fusion
  204.7 1.9 fusion.36
  209.6 24.7 %all-to-all-start.2 = ((f32[128,4,100]{2,1,0:T(4,128)}), f32[128,4,100]{2,1,0:T(4,128)S(1)}, u32[]{:S(2)}, u32[]{:S(2)}) async-start(f32[128,4,100]{2,1,0:T(4,128)} %bitcast.35), calls=%async_computation.2 | async-start | bytes 524288 | tf_op jit(solution)/shard_map/all_to_all | solution.py:126
  235.5 14.4 %all_gather.3 = bf16[8,100,512]{2,1,0:T(8,128)(2,1)S(1)} all-gather(bf16[2,100,512]{2,1,0:T(8,128)(2,1)S(1)} %copy.52), channel_id=1, replica_groups=mesh['mem'=4,'lat'=4,'lon'=32] {'mem'}, dimensions={0}, use_global_device_ids=true | all-gather | bytes 1024000 | tf_op jit(solution)/shard_map/all_gather | solution.py:131
  250.1 3.9 %fusion.33 = f32[8]{0:T(128)S(1)} fusion(f32[100,512,1]{1,2,0:T(1,128)S(1)} %copy.60, f32[8,100,512]{2,1,0:T(8,128)S(1)} %convert_multiply_fusion), kind=kOutput, calls=%fused_computation.37 | convolution fusion | flops 4915208 | bytes 1843232 | tf_op jit(solution)/shard_map/mks,ks->m/dot_general | solution.py:139
  254.0 2.6 fusion.27
  256.5 13.0 %all-reduce.1 = (f32[8,8]{1,0:T(8,128)S(1)}, f32[8]{0:T(128)S(1)}) all-reduce(f32[8,8]{1,0:T(8,128)S(1)} %fusion.27, f32[8]{0:T(128)S(1)} %fusion.33), channel_id=1, replica_groups=mesh['mem'=4,'lat'=4,'lon'=32] {'lat'}, use_global_device_ids=true, to_apply=%region_5.6 | all-reduce | flops 72 | bytes 576 | tf_op jit(solution)/shard_map/psum | solution.py:10
  269.5 79.6 %all-reduce = (f32[8,8]{1,0:T(8,128)}, f32[8]{0:T(128)}) all-reduce(f32[8,8]{1,0:T(8,128)S(1)} %get-tuple-element.22, f32[8]{0:T(128)S(1)} %get-tuple-element.23), channel_id=1, replica_groups=mesh['mem'=4,'lat'=4,'lon'=32] {'lon'}, use_global_device_ids=true, to_apply=%region_6.7 | all-reduce | flops 72 | bytes 576 | tf_op jit(solution)/shard_map/psum | solution.py:11
  (127 shorter events, 45.6 us)
Async XLA Ops:
  0.6 18.0 %copy-start = (f32[16,100]{1,0:T(8,128)S(1)}, f32[16,100]{1,0:T(8,128)}, u32[]{:S(2)}) copy-start(f32[16,100]{1,0:T(8,128)} %param.14) | copy-start | bytes 19204
  1.6 18.6 %collective-permute-start.1 = (bf16[3,100,1,128]{3,1,2,0:T(8,128)(2,1)S(1)}, bf16[3,100,1,128]{3,1,2,0:T(8,128)(2,1)S(1)}, u32[]{:S(2)}, u32[]{:S(2)}) collective-permute-start(bf16[3,100,1,128]{3,1,2,0:T(8,128)(2,1)S(1)} %broadcast_in_dim.30), channel_id=1, source_target_pairs={{1,0},{2,1},{3,2},{4,3},{5,4},{6,5},{7,6},{8,7},{9,8},{10,9},{11,1... | collective-permute-start | bytes 230408 | tf_op jit(solution)/shard_map/ppermute | solution.py:24
  15.6 10.2 %collective-permute-start = (bf16[3,100,1,128]{3,1,2,0:T(8,128)(2,1)S(1)}, bf16[3,100,1,128]{3,1,2,0:T(8,128)(2,1)S(1)}, u32[]{:S(2)}, u32[]{:S(2)}) collective-permute-start(bf16[3,100,1,128]{3,1,2,0:T(8,128)(2,1)S(1)} %broadcast_in_dim.28), channel_id=1, source_target_pairs={{0,1},{1,2},{2,3},{3,4},{4,5},{5,6},{6,7},{7,8},{8,9},{9,10},{10,1... | collective-permute-start | bytes 230408 | tf_op jit(solution)/shard_map/ppermute | solution.py:22
  18.4 10.5 %copy-start.10 = (s32[4,128]{1,0:T(4,128)S(1)}, s32[4,128]{1,0:T(4,128)}, u32[]{:S(2)}) copy-start(s32[4,128]{1,0:T(4,128)} %param.13) | copy-start | bytes 6148
  18.4 10.5 %copy-start.8 = (bf16[2,100,100]{2,0,1:T(2,128)(2,1)S(1)}, bf16[2,100,100]{2,0,1:T(2,128)(2,1)}, u32[]{:S(2)}) copy-start(bf16[2,100,100]{2,0,1:T(2,128)(2,1)} %param.17) | copy-start | bytes 120004
  26.2 9.0 %copy-start.11 = (bf16[100,100]{1,0:T(8,128)(2,1)S(1)}, bf16[100,100]{1,0:T(8,128)(2,1)}, u32[]{:S(2)}) copy-start(bf16[100,100]{1,0:T(8,128)(2,1)} %param.18) | copy-start | bytes 60004
  26.2 2.8 collective-permute-start.2
  27.5 7.1 %collective-permute-start.3 = (bf16[3,100,6,1]{3,1,2,0:T(8,128)(2,1)S(1)}, bf16[3,100,6,1]{3,1,2,0:T(8,128)(2,1)S(1)}, u32[]{:S(2)}, u32[]{:S(2)}) collective-permute-start(bf16[3,100,6,1]{3,1,2,0:T(8,128)(2,1)S(1)} %get-tuple-element.35), channel_id=1, source_target_pairs={{32,0},{64,32},{96,64},{33,1},{65,33},{97,65},{34,2},{66,34},{98,6... | collective-permute-start | bytes 10808 | tf_op jit(solution)/shard_map/ppermute | solution.py:24
  35.2 11.4 %copy-start.9 = (s32[256,1]{0,1:T(1,128)S(1)}, s32[256,1]{0,1:T(1,128)}, u32[]{:S(2)}) copy-start(s32[256,1]{0,1:T(1,128)} %param.19) | copy-start | bytes 3076
  36.8 10.2 %collective-permute-start.4 = (bf16[3,100,1,128]{3,1,2,0:T(8,128)(2,1)S(1)}, bf16[3,100,1,128]{3,1,2,0:T(8,128)(2,1)S(1)}, u32[]{:S(2)}, u32[]{:S(2)}) collective-permute-start(bf16[3,100,1,128]{3,1,2,0:T(8,128)(2,1)S(1)} %get-tuple-element.42), channel_id=1, source_target_pairs={{0,1},{1,2},{2,3},{3,4},{4,5},{5,6},{6,7},{7,8},{8,9},{9,10},{10,1... | collective-permute-start | bytes 230408 | tf_op jit(solution)/shard_map/ppermute | solution.py:22
  38.7 9.9 %collective-permute-start.5 = (bf16[3,100,1,128]{3,1,2,0:T(8,128)(2,1)S(1)}, bf16[3,100,1,128]{3,1,2,0:T(8,128)(2,1)S(1)}, u32[]{:S(2)}, u32[]{:S(2)}) collective-permute-start(bf16[3,100,1,128]{3,1,2,0:T(8,128)(2,1)S(1)} %get-tuple-element.43), channel_id=1, source_target_pairs={{1,0},{2,1},{3,2},{4,3},{5,4},{6,5},{7,6},{8,7},{9,8},{10,9},{11,1... | collective-permute-start | bytes 230408 | tf_op jit(solution)/shard_map/ppermute | solution.py:24
  48.9 29.6 %collective-permute-start.6 = (bf16[3,100,6,1]{3,1,2,0:T(8,128)(2,1)S(1)}, bf16[3,100,6,1]{3,1,2,0:T(8,128)(2,1)S(1)}, u32[]{:S(2)}, u32[]{:S(2)}) collective-permute-start(bf16[3,100,6,1]{3,1,2,0:T(8,128)(2,1)S(1)} %get-tuple-element.32), channel_id=1, source_target_pairs={{0,32},{32,64},{64,96},{1,33},{33,65},{65,97},{2,34},{34,66},{66,9... | collective-permute-start | bytes 10808 | tf_op jit(solution)/shard_map/ppermute | solution.py:22
  61.0 17.5 %collective-permute-start.7 = (bf16[3,100,6,1]{3,1,2,0:T(8,128)(2,1)S(1)}, bf16[3,100,6,1]{3,1,2,0:T(8,128)(2,1)S(1)}, u32[]{:S(2)}, u32[]{:S(2)}) collective-permute-start(bf16[3,100,6,1]{3,1,2,0:T(8,128)(2,1)S(1)} %get-tuple-element.33), channel_id=1, source_target_pairs={{32,0},{64,32},{96,64},{33,1},{65,33},{97,65},{34,2},{66,34},{98,6... | collective-permute-start | bytes 10808 | tf_op jit(solution)/shard_map/ppermute | solution.py:24
  64.6 52.8 %all-to-all-start.1 = ((s32[128,1,4]{2,1,0:T(1,128)}), s32[128,1,4]{2,1,0:T(1,128)S(1)}, u32[]{:S(2)}, u32[]{:S(2)}) async-start(s32[128,1,4]{2,1,0:T(1,128)} %bitcast.22), calls=%async_computation.1 | async-start | bytes 131072 | tf_op jit(solution)/shard_map/all_to_all | solution.py:102
  79.1 11.4 %copy-start.5 = (f32[256,100]{0,1:T(8,128)S(1)}, f32[256,100]{0,1:T(8,128)}, u32[]{:S(2)}) copy-start(f32[256,100]{0,1:T(8,128)} %param.23) | copy-start | bytes 307204
  79.1 11.4 %copy-start.6 = (f32[256,100]{0,1:T(8,128)S(1)}, f32[256,100]{0,1:T(8,128)}, u32[]{:S(2)}) copy-start(f32[256,100]{0,1:T(8,128)} %param.22) | copy-start | bytes 307204
  79.1 11.4 %copy-start.7 = (f32[256,100]{0,1:T(8,128)S(1)}, f32[256,100]{0,1:T(8,128)}, u32[]{:S(2)}) copy-start(f32[256,100]{0,1:T(8,128)} %param.21) | copy-start | bytes 307204
  80.7 10.3 %collective-permute-start.8 = (bf16[3,100,1,128]{3,1,2,0:T(8,128)(2,1)S(1)}, bf16[3,100,1,128]{3,1,2,0:T(8,128)(2,1)S(1)}, u32[]{:S(2)}, u32[]{:S(2)}) collective-permute-start(bf16[3,100,1,128]{3,1,2,0:T(8,128)(2,1)S(1)} %get-tuple-element.40), channel_id=1, source_target_pairs={{0,1},{1,2},{2,3},{3,4},{4,5},{5,6},{6,7},{7,8},{8,9},{9,10},{10,1... | collective-permute-start | bytes 230408 | tf_op jit(solution)/shard_map/ppermute | solution.py:22
  83.8 8.7 %collective-permute-start.9 = (bf16[3,100,1,128]{3,1,2,0:T(8,128)(2,1)S(1)}, bf16[3,100,1,128]{3,1,2,0:T(8,128)(2,1)S(1)}, u32[]{:S(2)}, u32[]{:S(2)}) collective-permute-start(bf16[3,100,1,128]{3,1,2,0:T(8,128)(2,1)S(1)} %get-tuple-element.41), channel_id=1, source_target_pairs={{1,0},{2,1},{3,2},{4,3},{5,4},{6,5},{7,6},{8,7},{9,8},{10,9},{11,1... | collective-permute-start | bytes 230408 | tf_op jit(solution)/shard_map/ppermute | solution.py:24
  93.7 11.4 %collective-permute-start.10 = (bf16[3,100,6,1]{3,1,2,0:T(8,128)(2,1)}, bf16[3,100,6,1]{3,1,2,0:T(8,128)(2,1)S(1)}, u32[]{:S(2)}, u32[]{:S(2)}) collective-permute-start(bf16[3,100,6,1]{3,1,2,0:T(8,128)(2,1)} %get-tuple-element.30), channel_id=1, source_target_pairs={{0,32},{32,64},{64,96},{1,33},{33,65},{65,97},{2,34},{34,66},{66,9... | collective-permute-start | bytes 10808 | tf_op jit(solution)/shard_map/ppermute | solution.py:22
  95.1 10.1 %collective-permute-start.11 = (bf16[3,100,6,1]{3,1,2,0:T(8,128)(2,1)}, bf16[3,100,6,1]{3,1,2,0:T(8,128)(2,1)S(1)}, u32[]{:S(2)}, u32[]{:S(2)}) collective-permute-start(bf16[3,100,6,1]{3,1,2,0:T(8,128)(2,1)} %get-tuple-element.31), channel_id=1, source_target_pairs={{32,0},{64,32},{96,64},{33,1},{65,33},{97,65},{34,2},{66,34},{98,6... | collective-permute-start | bytes 10808 | tf_op jit(solution)/shard_map/ppermute | solution.py:24
  107.3 31.9 %collective-permute-start.12 = (bf16[3,100,1,128]{3,1,2,0:T(8,128)(2,1)S(1)}, bf16[3,100,1,128]{3,1,2,0:T(8,128)(2,1)S(1)}, u32[]{:S(2)}, u32[]{:S(2)}) collective-permute-start(bf16[3,100,1,128]{3,1,2,0:T(8,128)(2,1)S(1)} %get-tuple-element.38), channel_id=1, source_target_pairs={{0,1},{1,2},{2,3},{3,4},{4,5},{5,6},{6,7},{7,8},{8,9},{9,10},{10,1... | collective-permute-start | bytes 230408 | tf_op jit(solution)/shard_map/ppermute | solution.py:22
  109.2 30.0 %collective-permute-start.13 = (bf16[3,100,1,128]{3,1,2,0:T(8,128)(2,1)S(1)}, bf16[3,100,1,128]{3,1,2,0:T(8,128)(2,1)S(1)}, u32[]{:S(2)}, u32[]{:S(2)}) collective-permute-start(bf16[3,100,1,128]{3,1,2,0:T(8,128)(2,1)S(1)} %get-tuple-element.39), channel_id=1, source_target_pairs={{1,0},{2,1},{3,2},{4,3},{5,4},{6,5},{7,6},{8,7},{9,8},{10,9},{11,1... | collective-permute-start | bytes 230408 | tf_op jit(solution)/shard_map/ppermute | solution.py:24
  117.5 86.9 %all-to-all-start = ((f32[128,4,3,100]{3,1,2,0:T(4,128)}), f32[128,4,3,100]{3,1,2,0:T(4,128)S(1)}, u32[]{:S(2)}, u32[]{:S(2)}) async-start(f32[128,4,3,100]{3,1,2,0:T(4,128)} %copy.47), calls=%async_computation | async-start | bytes 1572864 | tf_op jit(solution)/shard_map/all_to_all | solution.py:103
  139.5 3.3 collective-permute-start.14
  141.1 9.1 %collective-permute-start.15 = (bf16[3,100,6,1]{3,1,2,0:T(8,128)(2,1)S(1)}, bf16[3,100,6,1]{3,1,2,0:T(8,128)(2,1)}, u32[]{:S(2)}, u32[]{:S(2)}) collective-permute-start(bf16[3,100,6,1]{3,1,2,0:T(8,128)(2,1)S(1)} %get-tuple-element.29), channel_id=1, source_target_pairs={{32,0},{64,32},{96,64},{33,1},{65,33},{97,65},{34,2},{66,34},{98,6... | collective-permute-start | bytes 10808 | tf_op jit(solution)/shard_map/ppermute | solution.py:24
  153.6 11.6 %collective-permute-start.16 = (bf16[3,100,1,128]{3,1,2,0:T(8,128)(2,1)S(1)}, bf16[3,100,1,128]{3,1,2,0:T(8,128)(2,1)S(1)}, u32[]{:S(2)}, u32[]{:S(2)}) collective-permute-start(bf16[3,100,1,128]{3,1,2,0:T(8,128)(2,1)S(1)} %get-tuple-element.36), channel_id=1, source_target_pairs={{0,1},{1,2},{2,3},{3,4},{4,5},{5,6},{6,7},{7,8},{8,9},{9,10},{10,1... | collective-permute-start | bytes 230408 | tf_op jit(solution)/shard_map/ppermute | solution.py:22
  156.1 9.7 %collective-permute-start.17 = (bf16[3,100,1,128]{3,1,2,0:T(8,128)(2,1)S(1)}, bf16[3,100,1,128]{3,1,2,0:T(8,128)(2,1)S(1)}, u32[]{:S(2)}, u32[]{:S(2)}) collective-permute-start(bf16[3,100,1,128]{3,1,2,0:T(8,128)(2,1)S(1)} %get-tuple-element.37), channel_id=1, source_target_pairs={{1,0},{2,1},{3,2},{4,3},{5,4},{6,5},{7,6},{8,7},{9,8},{10,9},{11,1... | collective-permute-start | bytes 230408 | tf_op jit(solution)/shard_map/ppermute | solution.py:24
  166.0 25.3 %collective-permute-start.18 = (bf16[3,100,6,1]{3,1,2,0:T(8,128)(2,1)S(1)}, bf16[3,100,6,1]{3,1,2,0:T(8,128)(2,1)S(1)}, u32[]{:S(2)}, u32[]{:S(2)}) collective-permute-start(bf16[3,100,6,1]{3,1,2,0:T(8,128)(2,1)S(1)} %get-tuple-element.26), channel_id=1, source_target_pairs={{0,32},{32,64},{64,96},{1,33},{33,65},{65,97},{2,34},{34,66},{66,9... | collective-permute-start | bytes 10808 | tf_op jit(solution)/shard_map/ppermute | solution.py:22
  189.5 4.2 %collective-permute-start.19 = (bf16[3,100,6,1]{3,1,2,0:T(8,128)(2,1)S(1)}, bf16[3,100,6,1]{3,1,2,0:T(8,128)(2,1)}, u32[]{:S(2)}, u32[]{:S(2)}) collective-permute-start(bf16[3,100,6,1]{3,1,2,0:T(8,128)(2,1)S(1)} %get-tuple-element.27), channel_id=1, source_target_pairs={{32,0},{64,32},{96,64},{33,1},{65,33},{97,65},{34,2},{66,34},{98,6... | collective-permute-start | bytes 10808 | tf_op jit(solution)/shard_map/ppermute | solution.py:24
  201.7 1.9 slice-start
  209.6 139.5 %all-to-all-start.2 = ((f32[128,4,100]{2,1,0:T(4,128)}), f32[128,4,100]{2,1,0:T(4,128)S(1)}, u32[]{:S(2)}, u32[]{:S(2)}) async-start(f32[128,4,100]{2,1,0:T(4,128)} %bitcast.35), calls=%async_computation.2 | async-start | bytes 524288 | tf_op jit(solution)/shard_map/all_to_all | solution.py:126
  (4 other events, 3.5 us)
